TPU v7x, 128 devices: a whole 4x4x4 slice. The times are simulated.
128 devices in a mesh: seq: 32 (over z, x, core), head: 4 (over y).
Axes of the slice: x: 4, y: 4, z: 4, core: 2. Of those that a mesh axis runs over, the one named last changes fastest.
Arguments:
- inputs: bfloat16 [32768, 2048], P('seq', 'head'), may hold values from -6 to 6
- w_qkv: bfloat16 [3, 2048, 2048], P(None, None, 'head'), may hold values from -0.125 to 0.125
- level_weight: float32 [16, 6], P('head'), may hold values from 0.5 to 2
- grad_out: bfloat16 [32768, 2048], P('seq', 'head'), may hold values from -6 to 6
Outputs:
- attn_out: bfloat16 [32768, 2048], P('seq', 'head')
- grad_query: bfloat16 [32768, 2048], P('seq', 'head')
- grad_key: bfloat16 [32768, 2048], P('seq', 'head')
- grad_value: bfloat16 [32768, 2048], P('seq', 'head')
All inputs are finite; a program needn't handle non-finite values.
Results may differ from a plain program's by a relative error of at most 0.012.
Values may be sent and summed in bfloat16 or wider, within the bound.
A program may use at most 128 MiB of HBM per device.

v0:
```python
import math
import jax
import jax.numpy as jnp
from jax import lax
from jax.sharding import PartitionSpec as P


def partner(value, axis, stride):
    mask = 2**stride
    pairs = [(source, source ^ mask) for source in range(lax.axis_size(axis))]
    return lax.ppermute(value, axis, pairs)


def per_device(inputs, w_qkv, level_weight, grad_out):
    rows = inputs.shape[0]
    head_count = level_weight.shape[0]
    width = w_qkv.shape[2]
    head_size = width // head_count
    projected = jnp.einsum(
        "tn,jnf->jtf",
        lax.all_gather(inputs, "head", axis=1, tiled=True),
        w_qkv,
        preferred_element_type=jnp.float32,
    ).astype(jnp.bfloat16)
    queries = projected[0].reshape(rows, head_count, head_size)
    keys = projected[1].reshape(rows, head_count, head_size)
    values = projected[2].reshape(rows, head_count, head_size)
    grad_rows = grad_out.reshape(rows, head_count, head_size)
    key_state = jnp.einsum("thd,the->hde", keys, values, preferred_element_type=jnp.float32)
    query_state = jnp.einsum("thd,the->hde", queries, grad_rows, preferred_element_type=jnp.float32)
    position = lax.axis_index("seq")
    depth = lax.axis_size("seq").bit_length() - 1

    def level_coef(bit_level):
        return level_weight[:, bit_level + 1] / math.sqrt(head_size * rows * 2**bit_level)

    forward_mix = jnp.zeros((head_count, head_size, head_size), jnp.float32)
    backward_mix = jnp.zeros((head_count, head_size, head_size), jnp.float32)
    running = key_state
    for bit_level in range(depth):
        partner_sum = partner(running.astype(jnp.bfloat16), "seq", bit_level).astype(running.dtype)
        bit_on = position >> bit_level & 1 == 1
        forward_mix = forward_mix + jnp.where(
            bit_on, level_coef(bit_level)[:, None, None] * partner_sum, 0.0
        )
        running = running + partner_sum
    running = query_state
    for bit_level in range(depth):
        partner_sum = partner(running.astype(jnp.bfloat16), "seq", bit_level).astype(running.dtype)
        bit_on = position >> bit_level & 1 == 1
        backward_mix = backward_mix + jnp.where(
            bit_on, 0.0, level_coef(bit_level)[:, None, None] * partner_sum
        )
        running = running + partner_sum
    forward_low = forward_mix.astype(jnp.bfloat16)
    backward_low = backward_mix.astype(jnp.bfloat16)
    local_scale = (level_weight[:, 0] / math.sqrt(head_size * rows))[:, None, None]
    causal = (jnp.arange(rows)[:, None] >= jnp.arange(rows)[None, :])[None]
    scores = jnp.einsum("thd,shd->hts", queries, keys, preferred_element_type=jnp.float32)
    attend = jnp.where(causal, scores * local_scale, 0.0).astype(jnp.bfloat16)
    grad_scores = jnp.einsum("the,she->hts", grad_rows, values, preferred_element_type=jnp.float32)
    grad_attend = jnp.where(causal, grad_scores * local_scale, 0.0).astype(jnp.bfloat16)
    output = jnp.einsum("hts,she->the", attend, values, preferred_element_type=jnp.float32)
    output = output + jnp.einsum(
        "thd,hde->the", queries, forward_low, preferred_element_type=jnp.float32
    )
    grad_q = jnp.einsum("hts,shd->thd", grad_attend, keys, preferred_element_type=jnp.float32)
    grad_q = grad_q + jnp.einsum(
        "the,hde->thd", grad_rows, forward_low, preferred_element_type=jnp.float32
    )
    grad_k = jnp.einsum("hts,thd->shd", grad_attend, queries, preferred_element_type=jnp.float32)
    grad_k = grad_k + jnp.einsum(
        "the,hde->thd", values, backward_low, preferred_element_type=jnp.float32
    )
    grad_v = jnp.einsum("hts,the->she", attend, grad_rows, preferred_element_type=jnp.float32)
    grad_v = grad_v + jnp.einsum(
        "thd,hde->the", keys, backward_low, preferred_element_type=jnp.float32
    )
    return (
        output.reshape(rows, width).astype(jnp.bfloat16),
        grad_q.reshape(rows, width).astype(jnp.bfloat16),
        grad_k.reshape(rows, width).astype(jnp.bfloat16),
        grad_v.reshape(rows, width).astype(jnp.bfloat16),
    )


def solution(mesh):
    in_specs = (P("seq", "head"), P(None, None, "head"), P("head", None), P("seq", "head"))
    out_specs = (P("seq", "head"), P("seq", "head"), P("seq", "head"), P("seq", "head"))
    return jax.shard_map(
        per_device, mesh=mesh, in_specs=in_specs, out_specs=out_specs, check_vma=False
    )
```

profile of v0, /device:TPU:0, one launch (start us, length us, event | category | flops | bytes accessed | tf_op | source)
XLA Modules:
  0.0 144.0 jit_solution(12768049927329601054)
XLA Ops:
  9.4 1.6 %multiply_reduce_fusion.4 = (f32[4]{0:T(128)S(1)}, f32[4]{0:T(128)S(1)}, f32[4]{0:T(128)S(1)}, f32[4]{0:T(128)S(1)}, f32[4]{0:T(128)S(1)}, /*index=5*/f32[4]{0:T(128)}) fusion(f32[4,6]{1,0:T(4,128)} %param.6), kind=kLoop, calls=%fused_computation.56 | loop fusion | flops 24 | bytes 192 | tf_op jit(solution)/shard_map/div | solution.py:35
  12.3 48.1 %all-gather.2.cloned.1.call-done = bf16[1024,2048]{1,0:T(8,128)(2,1)} async-done(((bf16[1024,512]{1,0:T(8,128)(2,1)}), bf16[1024,2048]{1,0:T(8,128)(2,1)}) %all-gather.2.cloned.1.call-update) | async-done | bytes 4194320 | tf_op jit(solution)/shard_map/all_gather | solution.py:21
  60.4 10.3 %convert_bitcast_fusion = bf16[3,1024,512]{1,2,0:T(8,128)(2,1)S(1)} fusion(bf16[3,2048,512]{2,1,0:T(8,128)(2,1)} %param.5, bf16[1024,2048]{1,0:T(8,128)(2,1)} %all-gather.2.cloned.1.call-done), kind=kOutput, calls=%fused_computation.6 | convolution fusion | flops 6444023808 | bytes 13631488 | tf_op jit(solution)/shard_map/tn,jnf->jtf/dot_general | solution.py:19
  71.9 3.1 %fusion = bf16[4,1024,1024]{2,1,0:T(8,128)(2,1)S(1)} fusion(bf16[1024,4,128]{0,2,1:T(8,128)(2,1)S(1)} %bitcast.53, bf16[1024,4,128]{0,2,1:T(8,128)(2,1)S(1)} %bitcast.65, f32[4]{0:T(128)S(1)} %get-tuple-element.11, pred[1024,1024]{1,0:T(8,128)(4,1)S(1)} %copy-done.10), kind=kOutput, calls=%fused_computation.1 | convolution fusion | flops 1086324736 | bytes 11534352 | tf_op jit(solution)/shard_map/the,she->hts/dot_general | solution.py:61
  75.0 2.6 %fusion.42 = f32[4,128,1024]{2,1,0:T(8,128)} fusion(bf16[1024,4,128]{0,2,1:T(8,128)(2,1)S(1)} %bitcast.61, bf16[4,1024,1024]{2,1,0:T(8,128)(2,1)S(1)} %fusion), kind=kOutput, calls=%fused_computation.66 | convolution fusion | flops 1073741824 | bytes 11534336 | tf_op jit(solution)/shard_map/hts,thd->shd/dot_general | solution.py:71
  77.7 2.9 %fusion.41 = f32[4,128,1024]{2,1,0:T(8,128)S(1)} fusion(bf16[1024,4,128]{0,2,1:T(8,128)(2,1)S(1)} %bitcast.57, bf16[4,1024,1024]{2,1,0:T(8,128)(2,1)S(1)} %fusion), kind=kOutput, calls=%fused_computation.65 | convolution fusion | flops 1073741824 | bytes 11534336 | tf_op jit(solution)/shard_map/hts,shd->thd/dot_general | solution.py:67
  80.6 3.1 %select_convert_fusion = bf16[4,1024,1024]{2,1,0:T(8,128)(2,1)S(1)} fusion(bf16[1024,4,128]{0,2,1:T(8,128)(2,1)S(1)} %bitcast.62, bf16[1024,4,128]{0,2,1:T(8,128)(2,1)S(1)} %bitcast.58, f32[4]{0:T(128)S(1)} %get-tuple-element.11, pred[1024,1024]{1,0:T(8,128)(4,1)S(1)} %copy-done.10), kind=kOutput, calls=%fused_computation.2 | convolution fusion | flops 1086324736 | bytes 11534352 | tf_op jit(solution)/shard_map/thd,shd->hts/dot_general | solution.py:59
  84.3 4.3 %fusion.40 = f32[4,128,1024]{2,1,0:T(8,128)} fusion(bf16[1024,4,128]{0,2,1:T(8,128)(2,1)S(1)} %bitcast.66, bf16[4,1024,1024]{2,1,0:T(8,128)(2,1)S(1)} %select_convert_fusion), kind=kOutput, calls=%fused_computation.64 | convolution fusion | flops 1073741824 | bytes 11534336 | tf_op jit(solution)/shard_map/hts,she->the/dot_general | solution.py:63
  88.6 1.6 %collective-permute-start.1 = (bf16[4,128,128]{2,1,0:T(8,128)(2,1)S(1)}, bf16[4,128,128]{2,1,0:T(8,128)(2,1)S(1)}, u32[]{:S(2)}, u32[]{:S(2)}) collective-permute-start(bf16[4,128,128]{2,1,0:T(8,128)(2,1)S(1)} %fusion.26), channel_id=1, source_target_pairs={{0,8},{4,12},{8,0},{12,4},{16,24},{20,28},{24,16},{28,20},{32,40},... | collective-permute-start | bytes 393224 | tf_op jit(solution)/shard_map/ppermute | solution.py:11
  90.9 4.2 %collective-permute-done.1 = bf16[4,128,128]{2,1,0:T(8,128)(2,1)S(1)} collective-permute-done((bf16[4,128,128]{2,1,0:T(8,128)(2,1)S(1)}, bf16[4,128,128]{2,1,0:T(8,128)(2,1)S(1)}, u32[]{:S(2)}, u32[]{:S(2)}) %collective-permute-start.1) | collective-permute-done | bytes 131104 | tf_op jit(solution)/shard_map/ppermute | solution.py:11
  95.1 3.1 %collective-permute-start.2 = (bf16[4,128,128]{2,1,0:T(8,128)(2,1)S(1)}, bf16[4,128,128]{2,1,0:T(8,128)(2,1)S(1)}, u32[]{:S(2)}, u32[]{:S(2)}) collective-permute-start(bf16[4,128,128]{2,1,0:T(8,128)(2,1)S(1)} %fusion.30), channel_id=1, source_target_pairs={{0,16},{4,20},{8,24},{12,28},{16,0},{20,4},{24,8},{28,12},{32,48},... | collective-permute-start | bytes 393224 | tf_op jit(solution)/shard_map/ppermute | solution.py:11
  98.2 2.1 %collective-permute-start.7 = (bf16[4,128,128]{2,1,0:T(8,128)(2,1)S(1)}, bf16[4,128,128]{2,1,0:T(8,128)(2,1)S(1)}, u32[]{:S(2)}, u32[]{:S(2)}) collective-permute-start(bf16[4,128,128]{2,1,0:T(8,128)(2,1)S(1)} %fusion.31), channel_id=1, source_target_pairs={{0,16},{4,20},{8,24},{12,28},{16,0},{20,4},{24,8},{28,12},{32,48},... | collective-permute-start | bytes 393224 | tf_op jit(solution)/shard_map/ppermute | solution.py:11
  100.4 2.7 %collective-permute-done.2 = bf16[4,128,128]{2,1,0:T(8,128)(2,1)S(1)} collective-permute-done((bf16[4,128,128]{2,1,0:T(8,128)(2,1)S(1)}, bf16[4,128,128]{2,1,0:T(8,128)(2,1)S(1)}, u32[]{:S(2)}, u32[]{:S(2)}) %collective-permute-start.2) | collective-permute-done | bytes 131104 | tf_op jit(solution)/shard_map/ppermute | solution.py:11
  103.2 1.6 %collective-permute-start.3 = (bf16[4,128,128]{2,1,0:T(8,128)(2,1)S(1)}, bf16[4,128,128]{2,1,0:T(8,128)(2,1)S(1)}, u32[]{:S(2)}, u32[]{:S(2)}) collective-permute-start(bf16[4,128,128]{2,1,0:T(8,128)(2,1)S(1)} %fusion.27), channel_id=1, source_target_pairs={{0,32},{4,36},{8,40},{12,44},{16,48},{20,52},{24,56},{28,60},{32,0... | collective-permute-start | bytes 393224 | tf_op jit(solution)/shard_map/ppermute | solution.py:11
  105.0 1.6 %collective-permute-start.8 = (bf16[4,128,128]{2,1,0:T(8,128)(2,1)S(1)}, bf16[4,128,128]{2,1,0:T(8,128)(2,1)S(1)}, u32[]{:S(2)}, u32[]{:S(2)}) collective-permute-start(bf16[4,128,128]{2,1,0:T(8,128)(2,1)S(1)} %fusion.29), channel_id=1, source_target_pairs={{0,32},{4,36},{8,40},{12,44},{16,48},{20,52},{24,56},{28,60},{32,0... | collective-permute-start | bytes 393224 | tf_op jit(solution)/shard_map/ppermute | solution.py:11
  106.7 2.7 %collective-permute-done.3 = bf16[4,128,128]{2,1,0:T(8,128)(2,1)S(1)} collective-permute-done((bf16[4,128,128]{2,1,0:T(8,128)(2,1)S(1)}, bf16[4,128,128]{2,1,0:T(8,128)(2,1)S(1)}, u32[]{:S(2)}, u32[]{:S(2)}) %collective-permute-start.3) | collective-permute-done | bytes 131104 | tf_op jit(solution)/shard_map/ppermute | solution.py:11
  109.5 3.4 %collective-permute-start.4 = (bf16[4,128,128]{2,1,0:T(8,128)(2,1)S(1)}, bf16[4,128,128]{2,1,0:T(8,128)(2,1)S(1)}, u32[]{:S(2)}, u32[]{:S(2)}) collective-permute-start(bf16[4,128,128]{2,1,0:T(8,128)(2,1)S(1)} %fusion.15), channel_id=1, source_target_pairs={{0,64},{4,68},{8,72},{12,76},{16,80},{20,84},{24,88},{28,92},{32,9... | collective-permute-start | bytes 393224 | tf_op jit(solution)/shard_map/ppermute | solution.py:11
  113.7 2.4 %collective-permute-start.9 = (bf16[4,128,128]{2,1,0:T(8,128)(2,1)}, bf16[4,128,128]{2,1,0:T(8,128)(2,1)}, u32[]{:S(2)}, u32[]{:S(2)}) collective-permute-start(bf16[4,128,128]{2,1,0:T(8,128)(2,1)} %fusion.25), channel_id=1, source_target_pairs={{0,64},{4,68},{8,72},{12,76},{16,80},{20,84},{24,88},{28,92},{32,9... | collective-permute-start | bytes 393224 | tf_op jit(solution)/shard_map/ppermute | solution.py:11
  117.4 1.6 %add_convert_fusion.1 = bf16[4,128,1024]{2,1,0:T(8,128)(2,1)} fusion(f32[4,128,1024]{2,1,0:T(8,128)S(1)} %fusion.41, bf16[1024,4,128]{0,2,1:T(8,128)(2,1)S(1)} %bitcast.54, bf16[4,128,128]{2,1,0:T(8,128)(2,1)S(1)} %collective-permute-done, bf16[4,128,128]{2,1,0:T(8,128)(2,1)S(1)} %collective-permute-done.1, ...), kind=kOutput, calls=%fused_computation.10 | convolution fusion | flops 136577024 | bytes 4849749 | tf_op jit(solution)/shard_map/the,hde->thd/dot_general | solution.py:68
  119.0 2.3 %copy.25 = bf16[1024,512]{1,0:T(8,128)(2,1)} copy(bf16[1024,512]{0,1:T(8,128)(2,1)} %bitcast.71) | data formatting | bytes 2097152
  121.3 3.7 %add_convert_fusion = bf16[4,128,1024]{2,1,0:T(8,128)(2,1)} fusion(f32[4,128,1024]{2,1,0:T(8,128)} %fusion.42, bf16[1024,4,128]{0,2,1:T(8,128)(2,1)} %bitcast.67, bf16[4,128,128]{2,1,0:T(8,128)(2,1)S(1)} %collective-permute-done.5, bf16[4,128,128]{2,1,0:T(8,128)(2,1)} %copy-done.3, bf16[4,128,128]{2,1,0:T(8,128)(2,1)} %copy-done.6, ...), kind=kOutput, calls=%fused_computation.9 | convolution fusion | flops 136577024 | bytes 4849749 | tf_op jit(solution)/shard_map/the,hde->thd/dot_general | solution.py:72
  125.0 2.3 %copy.26 = bf16[1024,512]{1,0:T(8,128)(2,1)} copy(bf16[1024,512]{0,1:T(8,128)(2,1)} %bitcast.70) | data formatting | bytes 2097152
  127.3 1.7 %fusion.35 = f32[4,128,1024]{2,1,0:T(8,128)S(1)} fusion(bf16[1024,4,128]{0,2,1:T(8,128)(2,1)S(1)} %bitcast.59, bf16[4,128,128]{2,1,0:T(8,128)(2,1)S(1)} %collective-permute-done.5, bf16[4,128,128]{2,1,0:T(8,128)(2,1)} %copy-done.3, bf16[4,128,128]{2,1,0:T(8,128)(2,1)} %copy-done.6, bf16[4,128,128]{2,1,0:T(8,128)(2,1)} %copy-done.9, ...), kind=kOutput, calls=%fused_computation.63 | convolution fusion | flops 135528448 | bytes 3801173 | tf_op jit(solution)/shard_map/thd,hde->the/dot_general | solution.py:76
  129.0 4.8 %fusion.5 = bf16[1024,4,128]{0,2,1:T(8,128)(2,1)S(1)} fusion(f32[4,128,1024]{2,1,0:T(8,128)S(1)} %fusion.35, bf16[1024,4,128]{0,2,1:T(8,128)(2,1)S(1)} %bitcast.55, bf16[4,1024,1024]{2,1,0:T(8,128)(2,1)} %copy-done), kind=kOutput, calls=%fused_computation.8 | convolution fusion | flops 1074790400 | bytes 12582912 | tf_op jit(solution)/shard_map/hts,the->she/dot_general | solution.py:75
  (58 shorter events, 11.9 us)
Async XLA Ops:
  7.2 53.2 %all-gather.2.cloned.1.call-start = ((), (), s32[]{:S(2)}) async-start(), calls=%async_computation | async-start | bytes 5242880 | tf_op jit(solution)/shard_map/all_gather | solution.py:21
  71.0 13.3 %copy-start.1 = (bf16[1,1024,512]{1,2,0:T(8,128)(2,1)}, bf16[1,1024,512]{1,2,0:T(8,128)(2,1)S(1)}, u32[]{:S(2)}) copy-start(bf16[1,1024,512]{1,2,0:T(8,128)(2,1)S(1)} %get-tuple-element.16) | copy-start | bytes 3145732
  83.7 6.5 %copy-start = (bf16[4,1024,1024]{2,1,0:T(8,128)(2,1)}, bf16[4,1024,1024]{2,1,0:T(8,128)(2,1)S(1)}, u32[]{:S(2)}) copy-start(bf16[4,1024,1024]{2,1,0:T(8,128)(2,1)S(1)} %select_convert_fusion) | copy-start | bytes 25165828
  83.7 4.9 %collective-permute-start = (bf16[4,128,128]{2,1,0:T(8,128)(2,1)S(1)}, bf16[4,128,128]{2,1,0:T(8,128)(2,1)S(1)}, u32[]{:S(2)}, u32[]{:S(2)}) collective-permute-start(bf16[4,128,128]{2,1,0:T(8,128)(2,1)S(1)} %get-tuple-element.17), channel_id=1, source_target_pairs={{0,4},{4,0},{8,12},{12,8},{16,20},{20,16},{24,28},{28,24},{32,36},... | collective-permute-start | bytes 393224 | tf_op jit(solution)/shard_map/ppermute | solution.py:11
  83.8 33.6 %copy-start.13 = (f32[4]{0:T(128)S(1)}, f32[4]{0:T(128)}, u32[]{:S(2)}) copy-start(f32[4]{0:T(128)} %get-tuple-element.13) | copy-start | bytes 52
  83.8 6.4 %collective-permute-start.5 = (bf16[4,128,128]{2,1,0:T(8,128)(2,1)S(1)}, bf16[4,128,128]{2,1,0:T(8,128)(2,1)S(1)}, u32[]{:S(2)}, u32[]{:S(2)}) collective-permute-start(bf16[4,128,128]{2,1,0:T(8,128)(2,1)S(1)} %get-tuple-element.19), channel_id=1, source_target_pairs={{0,4},{4,0},{8,12},{12,8},{16,20},{20,16},{24,28},{28,24},{32,36},... | collective-permute-start | bytes 393224 | tf_op jit(solution)/shard_map/ppermute | solution.py:11
  88.6 6.5 %collective-permute-start.1 = (bf16[4,128,128]{2,1,0:T(8,128)(2,1)S(1)}, bf16[4,128,128]{2,1,0:T(8,128)(2,1)S(1)}, u32[]{:S(2)}, u32[]{:S(2)}) collective-permute-start(bf16[4,128,128]{2,1,0:T(8,128)(2,1)S(1)} %fusion.26), channel_id=1, source_target_pairs={{0,8},{4,12},{8,0},{12,4},{16,24},{20,28},{24,16},{28,20},{32,40},... | collective-permute-start | bytes 393224 | tf_op jit(solution)/shard_map/ppermute | solution.py:11
  90.2 8.0 %collective-permute-start.6 = (bf16[4,128,128]{2,1,0:T(8,128)(2,1)S(1)}, bf16[4,128,128]{2,1,0:T(8,128)(2,1)S(1)}, u32[]{:S(2)}, u32[]{:S(2)}) collective-permute-start(bf16[4,128,128]{2,1,0:T(8,128)(2,1)S(1)} %fusion.28), channel_id=1, source_target_pairs={{0,8},{4,12},{8,0},{12,4},{16,24},{20,28},{24,16},{28,20},{32,40},... | collective-permute-start | bytes 393224 | tf_op jit(solution)/shard_map/ppermute | solution.py:11
  95.1 8.0 %collective-permute-start.2 = (bf16[4,128,128]{2,1,0:T(8,128)(2,1)S(1)}, bf16[4,128,128]{2,1,0:T(8,128)(2,1)S(1)}, u32[]{:S(2)}, u32[]{:S(2)}) collective-permute-start(bf16[4,128,128]{2,1,0:T(8,128)(2,1)S(1)} %fusion.30), channel_id=1, source_target_pairs={{0,16},{4,20},{8,24},{12,28},{16,0},{20,4},{24,8},{28,12},{32,48},... | collective-permute-start | bytes 393224 | tf_op jit(solution)/shard_map/ppermute | solution.py:11
  98.2 20.8 %copy-start.3 = (bf16[4,128,128]{2,1,0:T(8,128)(2,1)}, bf16[4,128,128]{2,1,0:T(8,128)(2,1)S(1)}, u32[]{:S(2)}) copy-start(bf16[4,128,128]{2,1,0:T(8,128)(2,1)S(1)} %collective-permute-done.6) | copy-start | bytes 393220
  98.2 6.7 %collective-permute-start.7 = (bf16[4,128,128]{2,1,0:T(8,128)(2,1)S(1)}, bf16[4,128,128]{2,1,0:T(8,128)(2,1)S(1)}, u32[]{:S(2)}, u32[]{:S(2)}) collective-permute-start(bf16[4,128,128]{2,1,0:T(8,128)(2,1)S(1)} %fusion.31), channel_id=1, source_target_pairs={{0,16},{4,20},{8,24},{12,28},{16,0},{20,4},{24,8},{28,12},{32,48},... | collective-permute-start | bytes 393224 | tf_op jit(solution)/shard_map/ppermute | solution.py:11
  103.1 15.9 %copy-start.4 = (bf16[4,128,128]{2,1,0:T(8,128)(2,1)}, bf16[4,128,128]{2,1,0:T(8,128)(2,1)S(1)}, u32[]{:S(2)}) copy-start(bf16[4,128,128]{2,1,0:T(8,128)(2,1)S(1)} %collective-permute-done.2) | copy-start | bytes 393220
  103.2 6.2 %collective-permute-start.3 = (bf16[4,128,128]{2,1,0:T(8,128)(2,1)S(1)}, bf16[4,128,128]{2,1,0:T(8,128)(2,1)S(1)}, u32[]{:S(2)}, u32[]{:S(2)}) collective-permute-start(bf16[4,128,128]{2,1,0:T(8,128)(2,1)S(1)} %fusion.27), channel_id=1, source_target_pairs={{0,32},{4,36},{8,40},{12,44},{16,48},{20,52},{24,56},{28,60},{32,0... | collective-permute-start | bytes 393224 | tf_op jit(solution)/shard_map/ppermute | solution.py:11
  105.0 14.0 %copy-start.6 = (bf16[4,128,128]{2,1,0:T(8,128)(2,1)}, bf16[4,128,128]{2,1,0:T(8,128)(2,1)S(1)}, u32[]{:S(2)}) copy-start(bf16[4,128,128]{2,1,0:T(8,128)(2,1)S(1)} %collective-permute-done.7) | copy-start | bytes 393220
  105.0 7.9 %collective-permute-start.8 = (bf16[4,128,128]{2,1,0:T(8,128)(2,1)S(1)}, bf16[4,128,128]{2,1,0:T(8,128)(2,1)S(1)}, u32[]{:S(2)}, u32[]{:S(2)}) collective-permute-start(bf16[4,128,128]{2,1,0:T(8,128)(2,1)S(1)} %fusion.29), channel_id=1, source_target_pairs={{0,32},{4,36},{8,40},{12,44},{16,48},{20,52},{24,56},{28,60},{32,0... | collective-permute-start | bytes 393224 | tf_op jit(solution)/shard_map/ppermute | solution.py:11
  109.4 9.6 %copy-start.7 = (bf16[4,128,128]{2,1,0:T(8,128)(2,1)}, bf16[4,128,128]{2,1,0:T(8,128)(2,1)S(1)}, u32[]{:S(2)}) copy-start(bf16[4,128,128]{2,1,0:T(8,128)(2,1)S(1)} %collective-permute-done.3) | copy-start | bytes 393220
  109.5 7.9 %collective-permute-start.4 = (bf16[4,128,128]{2,1,0:T(8,128)(2,1)S(1)}, bf16[4,128,128]{2,1,0:T(8,128)(2,1)S(1)}, u32[]{:S(2)}, u32[]{:S(2)}) collective-permute-start(bf16[4,128,128]{2,1,0:T(8,128)(2,1)S(1)} %fusion.15), channel_id=1, source_target_pairs={{0,64},{4,68},{8,72},{12,76},{16,80},{20,84},{24,88},{28,92},{32,9... | collective-permute-start | bytes 393224 | tf_op jit(solution)/shard_map/ppermute | solution.py:11
  112.9 6.1 %copy-start.9 = (bf16[4,128,128]{2,1,0:T(8,128)(2,1)}, bf16[4,128,128]{2,1,0:T(8,128)(2,1)S(1)}, u32[]{:S(2)}) copy-start(bf16[4,128,128]{2,1,0:T(8,128)(2,1)S(1)} %collective-permute-done.8) | copy-start | bytes 393220
  113.7 7.6 %collective-permute-start.9 = (bf16[4,128,128]{2,1,0:T(8,128)(2,1)}, bf16[4,128,128]{2,1,0:T(8,128)(2,1)}, u32[]{:S(2)}, u32[]{:S(2)}) collective-permute-start(bf16[4,128,128]{2,1,0:T(8,128)(2,1)} %fusion.25), channel_id=1, source_target_pairs={{0,64},{4,68},{8,72},{12,76},{16,80},{20,84},{24,88},{28,92},{32,9... | collective-permute-start | bytes 393224 | tf_op jit(solution)/shard_map/ppermute | solution.py:11
  129.0 4.9 %copy-start.2 = (f32[4,128,1024]{2,1,0:T(8,128)S(1)}, f32[4,128,1024]{2,1,0:T(8,128)}, u32[]{:S(2)}) copy-start(f32[4,128,1024]{2,1,0:T(8,128)} %fusion.40) | copy-start | bytes 6291460
  129.0 4.9 %copy-start.5 = (bf16[4,128,128]{2,1,0:T(8,128)(2,1)S(1)}, bf16[4,128,128]{2,1,0:T(8,128)(2,1)}, u32[]{:S(2)}) copy-start(bf16[4,128,128]{2,1,0:T(8,128)(2,1)} %copy-done.4) | copy-start | bytes 393220
  129.0 4.9 %copy-start.8 = (bf16[4,128,128]{2,1,0:T(8,128)(2,1)S(1)}, bf16[4,128,128]{2,1,0:T(8,128)(2,1)}, u32[]{:S(2)}) copy-start(bf16[4,128,128]{2,1,0:T(8,128)(2,1)} %copy-done.7) | copy-start | bytes 393220
  129.0 4.9 %copy-start.12 = (bf16[4,128,128]{2,1,0:T(8,128)(2,1)S(1)}, bf16[4,128,128]{2,1,0:T(8,128)(2,1)}, u32[]{:S(2)}) copy-start(bf16[4,128,128]{2,1,0:T(8,128)(2,1)} %copy-done.11) | copy-start | bytes 393220
  129.0 4.9 %copy-start.14 = (f32[4]{0:T(128)S(1)}, f32[4]{0:T(128)}, u32[]{:S(2)}) copy-start(f32[4]{0:T(128)} %get-tuple-element.13) | copy-start | bytes 52
  (2 other events, 2.8 us)
Sparse Core Ops, SparseCore 0:
  9.6 50.7 all-gather.1
where the time goes:
time: 144 us
  waiting for transfers between devices  60 us (42%)
  matrix products  39.6 us (28%)
  starting transfers between devices  17.1 us (12%)
  between operations  14.3 us (10%)
  local copies, waits for them, and re-layouts  9.05 us (6%)
  other arithmetic  4.03 us (3%)
    all_gather x1, waiting for transfers between devices, per_device(): lax.all_gather(inputs, 'head', axis=1, tiled=True)  48.1 us
    ppermute x10, starting transfers between devices, partner(): return lax.ppermute(value, axis, pairs)  17 us
    ppermute x10, waiting for transfers between devices, partner(): return lax.ppermute(value, axis, pairs)  11.2 us
    dot_general x1, matrix products, per_device(): jnp.einsum('tn,jnf->jtf', lax.all_gather(inputs, 'head', axis=1, tiled=Tr...  10.3 us
    unnamed x34, local copies, waits for them, and re-layouts  7.26 us
    dot_general x1, matrix products, per_device(): jnp.einsum('hts,the->she', attend, grad_rows, preferred_element_type=jnp....  4.81 us
    dot_general x1, matrix products, per_device(): jnp.einsum('hts,she->the', attend, values, preferred_element_type=jnp.flo...  4.29 us
    dot_general x1, matrix products, per_device(): jnp.einsum('the,hde->thd', values, backward_low, preferred_element_type=j...  3.73 us
  transfers between devices with their start and end apart: 11, of which 6 were waited for; matrix products, arithmetic and copies ran while one was open for 9% of the time, Pallas kernels for 0%

commit v1 on v0

--- a/solution.py
+++ b/solution.py
@@ -18,7 +18,9 @@
     head_size = width // head_count
     projected = jnp.einsum(
         "tn,jnf->jtf",
-        lax.all_gather(inputs, "head", axis=1, tiled=True),
+        jnp.concatenate(
+            lax.all_to_all(jnp.stack([inputs] * lax.axis_size("head")), "head", 0, 0), axis=1
+        ),
         w_qkv,
         preferred_element_type=jnp.float32,
     ).astype(jnp.bfloat16)

time: 144 us -> 151 us (1.049)
  local copies, waits for them, and re-layouts: 9.05 us -> 26.8 us
  between operations: 14.3 us -> 0.88 us
  starting transfers between devices: 17.1 us -> 23.7 us
  waiting for transfers between devices: 60 us -> 57.9 us
    all_gather x1 -> x0, waiting for transfers between devices: 48.1 us -> none  [per_device(): lax.all_gather(inputs, 'head', axis=1, tiled=True)]
    all_to_all x0 -> x1, waiting for transfers between devices: none -> 46.5 us  [per_device(): lax.all_to_all(jnp.stack([inputs] * lax.axis_size('head')), 'head', 0, 0)]
    reshape x0 -> x2, local copies, waits for them, and re-layouts: none -> 15.1 us  [per_device(): jnp.concatenate(lax.all_to_all(jnp.stack([inputs] * lax.axis_size('head')...]
    all_to_all x0 -> x1, starting transfers between devices: none -> 4.97 us  [per_device(): lax.all_to_all(jnp.stack([inputs] * lax.axis_size('head')), 'head', 0, 0)]
    another operation x0 -> x1, local copies, waits for them, and re-layouts: none -> 3.53 us  [per_device(): jnp.stack([inputs] * lax.axis_size('head'))]
    dot_general x1, matrix products: 4.81 us -> 2.37 us  [per_device(): jnp.einsum('hts,the->she', attend, grad_rows, preferred_element_type=jnp....]
    ppermute x10, starting transfers between devices: 17 us -> 18.7 us  [partner(): return lax.ppermute(value, axis, pairs)]
  transfers between devices with their start and end apart: 11 -> 11, of which waited for: 6 -> 5; matrix products, arithmetic and copies ran while one was open for 9% -> 6% of each run, Pallas kernels for 0% -> 0%
where the time goes in v1:
time: 151 us
  waiting for transfers between devices  57.9 us (38%)
  matrix products  39.1 us (26%)
  local copies, waits for them, and re-layouts  26.8 us (18%)
  starting transfers between devices  23.7 us (16%)
  other arithmetic  2.53 us (2%)
    all_to_all x1, waiting for transfers between devices, per_device(): lax.all_to_all(jnp.stack([inputs] * lax.axis_size('head')), 'head', 0, 0)  46.5 us
    ppermute x10, starting transfers between devices, partner(): return lax.ppermute(value, axis, pairs)  18.7 us
    reshape x2, local copies, waits for them, and re-layouts, per_device(): jnp.concatenate(lax.all_to_all(jnp.stack([inputs] * lax.axis_size('head')...  15.1 us
    ppermute x10, waiting for transfers between devices, partner(): return lax.ppermute(value, axis, pairs)  11.4 us
    dot_general x1, matrix products, per_device(): jnp.einsum('tn,jnf->jtf', jnp.concatenate(lax.all_to_all(jnp.stack([input...  10.3 us
    unnamed x34, local copies, waits for them, and re-layouts  7.26 us
    all_to_all x1, starting transfers between devices, per_device(): lax.all_to_all(jnp.stack([inputs] * lax.axis_size('head')), 'head', 0, 0)  4.97 us
    dot_general x1, matrix products, per_device(): jnp.einsum('the,she->hts', grad_rows, values, preferred_element_type=jnp....  4.28 us
  transfers between devices with their start and end apart: 11, of which 5 were waited for; matrix products, arithmetic and copies ran while one was open for 6% of the time, Pallas kernels for 0%

profile of v1, /device:TPU:0, one launch (start us, length us, event | category | flops | bytes accessed | tf_op | source)
XLA Modules:
  0.0 150.9 jit_solution(5113017982983519478)
XLA Ops:
  0.6 3.5 %stack.2 = bf16[4,1024,512]{2,1,0:T(8,128)(2,1)} broadcast(bf16[1024,512]{1,0:T(8,128)(2,1)} %param.4), dimensions={1,2} | broadcast | bytes 5242880 | tf_op jit(solution)/shard_map/stack | solution.py:22
  4.2 5.0 %all-to-all-start = ((bf16[4,1024,512]{2,1,0:T(8,128)(2,1)}), bf16[4,1024,512]{2,1,0:T(8,128)(2,1)}, u32[]{:S(2)}, u32[]{:S(2)}) async-start(bf16[4,1024,512]{2,1,0:T(8,128)(2,1)} %stack.2), calls=%async_computation | async-start | bytes 8388608 | tf_op jit(solution)/shard_map/all_to_all | solution.py:22
  11.8 46.5 %all-to-all-done = bf16[4,1024,512]{2,1,0:T(8,128)(2,1)} async-done(((bf16[4,1024,512]{2,1,0:T(8,128)(2,1)}), bf16[4,1024,512]{2,1,0:T(8,128)(2,1)}, u32[]{:S(2)}, u32[]{:S(2)}) %all-to-all-start) | async-done | bytes 4194336 | tf_op jit(solution)/shard_map/all_to_all | solution.py:22
  58.3 7.4 %copy.28 = bf16[1024,4,512]{2,1,0:T(4,128)(2,1)} copy(bf16[1024,4,512]{2,0,1:T(8,128)(2,1)} %bitcast) | data formatting | bytes 8388608 | tf_op jit(solution)/shard_map/reshape | solution.py:21
  65.7 7.7 %reshape.84 = bf16[1024,2048,1]{1,0,2:T(8,128)(2,1)} reshape(bf16[1024,4,512]{2,1,0:T(4,128)(2,1)} %copy.28) | data formatting | bytes 8388608 | tf_op jit(solution)/shard_map/reshape | solution.py:21
  73.5 10.3 %convert_bitcast_fusion = bf16[3,1024,512]{1,2,0:T(8,128)(2,1)S(1)} fusion(bf16[3,2048,512]{2,1,0:T(8,128)(2,1)} %param.5, bf16[1024,2048,1]{1,0,2:T(8,128)(2,1)} %reshape.84), kind=kOutput, calls=%fused_computation.4 | convolution fusion | flops 6444023808 | bytes 13631488 | tf_op jit(solution)/shard_map/tn,jnf->jtf/dot_general | solution.py:19
  86.4 3.1 %select_convert_fusion = bf16[4,1024,1024]{2,1,0:T(8,128)(2,1)S(1)} fusion(bf16[1024,4,128]{0,2,1:T(8,128)(2,1)S(1)} %bitcast.62, bf16[1024,4,128]{0,2,1:T(8,128)(2,1)S(1)} %bitcast.54, f32[4]{0:T(128)S(1)} %get-tuple-element.15, pred[1024,1024]{1,0:T(8,128)(4,1)S(1)} %copy-done.8), kind=kOutput, calls=%fused_computation.2 | convolution fusion | flops 1086324736 | bytes 11534352 | tf_op jit(solution)/shard_map/thd,shd->hts/dot_general | solution.py:61
  89.5 4.3 %fusion = bf16[4,1024,1024]{2,1,0:T(8,128)(2,1)S(1)} fusion(bf16[1024,4,128]{0,2,1:T(8,128)(2,1)S(1)} %bitcast.50, bf16[1024,4,128]{0,2,1:T(8,128)(2,1)S(1)} %bitcast.58, f32[4]{0:T(128)S(1)} %get-tuple-element.15, pred[1024,1024]{1,0:T(8,128)(4,1)} %iota_compare_fusion), kind=kOutput, calls=%fused_computation.1 | convolution fusion | flops 1086324736 | bytes 11534352 | tf_op jit(solution)/shard_map/the,she->hts/dot_general | solution.py:63
  93.8 2.6 %fusion.38 = f32[4,128,1024]{2,1,0:T(8,128)} fusion(bf16[1024,4,128]{0,2,1:T(8,128)(2,1)S(1)} %bitcast.63, bf16[4,1024,1024]{2,1,0:T(8,128)(2,1)S(1)} %fusion), kind=kOutput, calls=%fused_computation.64 | convolution fusion | flops 1073741824 | bytes 11534336 | tf_op jit(solution)/shard_map/hts,thd->shd/dot_general | solution.py:73
  96.4 4.2 %fusion.37 = f32[4,128,1024]{2,1,0:T(8,128)} fusion(bf16[1024,4,128]{0,2,1:T(8,128)(2,1)S(1)} %bitcast.55, bf16[4,1024,1024]{2,1,0:T(8,128)(2,1)S(1)} %fusion), kind=kOutput, calls=%fused_computation.63 | convolution fusion | flops 1073741824 | bytes 11534336 | tf_op jit(solution)/shard_map/hts,shd->thd/dot_general | solution.py:69
  101.2 2.9 %fusion.36 = f32[4,128,1024]{2,1,0:T(8,128)S(1)} fusion(bf16[1024,4,128]{0,2,1:T(8,128)(2,1)S(1)} %bitcast.59, bf16[4,1024,1024]{2,1,0:T(8,128)(2,1)S(1)} %select_convert_fusion), kind=kOutput, calls=%fused_computation.62 | convolution fusion | flops 1073741824 | bytes 11534336 | tf_op jit(solution)/shard_map/hts,she->the/dot_general | solution.py:65
  106.4 4.2 %collective-permute-done.6 = bf16[4,128,128]{2,1,0:T(8,128)(2,1)S(1)} collective-permute-done((bf16[4,128,128]{2,1,0:T(8,128)(2,1)S(1)}, bf16[4,128,128]{2,1,0:T(8,128)(2,1)S(1)}, u32[]{:S(2)}, u32[]{:S(2)}) %collective-permute-start.6) | collective-permute-done | bytes 131104 | tf_op jit(solution)/shard_map/ppermute | solution.py:11
  110.7 3.1 %collective-permute-start.7 = (bf16[4,128,128]{2,1,0:T(8,128)(2,1)S(1)}, bf16[4,128,128]{2,1,0:T(8,128)(2,1)S(1)}, u32[]{:S(2)}, u32[]{:S(2)}) collective-permute-start(bf16[4,128,128]{2,1,0:T(8,128)(2,1)S(1)} %fusion.27), channel_id=1, source_target_pairs={{0,16},{4,20},{8,24},{12,28},{16,0},{20,4},{24,8},{28,12},{32,48},... | collective-permute-start | bytes 393224 | tf_op jit(solution)/shard_map/ppermute | solution.py:11
  113.9 2.1 %collective-permute-start.2 = (bf16[4,128,128]{2,1,0:T(8,128)(2,1)S(1)}, bf16[4,128,128]{2,1,0:T(8,128)(2,1)S(1)}, u32[]{:S(2)}, u32[]{:S(2)}) collective-permute-start(bf16[4,128,128]{2,1,0:T(8,128)(2,1)S(1)} %fusion.26), channel_id=1, source_target_pairs={{0,16},{4,20},{8,24},{12,28},{16,0},{20,4},{24,8},{28,12},{32,48},... | collective-permute-start | bytes 393224 | tf_op jit(solution)/shard_map/ppermute | solution.py:11
  116.0 2.6 %collective-permute-done.7 = bf16[4,128,128]{2,1,0:T(8,128)(2,1)S(1)} collective-permute-done((bf16[4,128,128]{2,1,0:T(8,128)(2,1)S(1)}, bf16[4,128,128]{2,1,0:T(8,128)(2,1)S(1)}, u32[]{:S(2)}, u32[]{:S(2)}) %collective-permute-start.7) | collective-permute-done | bytes 131104 | tf_op jit(solution)/shard_map/ppermute | solution.py:11
  122.7 2.3 %collective-permute-done.8 = bf16[4,128,128]{2,1,0:T(8,128)(2,1)S(1)} collective-permute-done((bf16[4,128,128]{2,1,0:T(8,128)(2,1)S(1)}, bf16[4,128,128]{2,1,0:T(8,128)(2,1)S(1)}, u32[]{:S(2)}, u32[]{:S(2)}) %collective-permute-start.8) | collective-permute-done | bytes 131104 | tf_op jit(solution)/shard_map/ppermute | solution.py:11
  125.1 4.2 %collective-permute-start.9 = (bf16[4,128,128]{2,1,0:T(8,128)(2,1)S(1)}, bf16[4,128,128]{2,1,0:T(8,128)(2,1)S(1)}, u32[]{:S(2)}, u32[]{:S(2)}) collective-permute-start(bf16[4,128,128]{2,1,0:T(8,128)(2,1)S(1)} %fusion.21), channel_id=1, source_target_pairs={{0,64},{4,68},{8,72},{12,76},{16,80},{20,84},{24,88},{28,92},{32,9... | collective-permute-start | bytes 393224 | tf_op jit(solution)/shard_map/ppermute | solution.py:11
  129.4 2.7 %collective-permute-start.4 = (bf16[4,128,128]{2,1,0:T(8,128)(2,1)S(1)}, bf16[4,128,128]{2,1,0:T(8,128)(2,1)S(1)}, u32[]{:S(2)}, u32[]{:S(2)}) collective-permute-start(bf16[4,128,128]{2,1,0:T(8,128)(2,1)S(1)} %fusion.11), channel_id=1, source_target_pairs={{0,64},{4,68},{8,72},{12,76},{16,80},{20,84},{24,88},{28,92},{32,9... | collective-permute-start | bytes 393224 | tf_op jit(solution)/shard_map/ppermute | solution.py:11
  132.0 2.2 %collective-permute-done.9 = bf16[4,128,128]{2,1,0:T(8,128)(2,1)S(1)} collective-permute-done((bf16[4,128,128]{2,1,0:T(8,128)(2,1)S(1)}, bf16[4,128,128]{2,1,0:T(8,128)(2,1)S(1)}, u32[]{:S(2)}, u32[]{:S(2)}) %collective-permute-start.9) | collective-permute-done | bytes 131104 | tf_op jit(solution)/shard_map/ppermute | solution.py:11
  134.9 2.4 %fusion.1 = bf16[1024,4,128]{0,2,1:T(8,128)(2,1)} fusion(f32[4,128,1024]{2,1,0:T(8,128)S(1)} %fusion.31, bf16[1024,4,128]{0,2,1:T(8,128)(2,1)S(1)} %bitcast.51, bf16[4,1024,1024]{2,1,0:T(8,128)(2,1)S(1)} %select_convert_fusion), kind=kOutput, calls=%fused_computation.6 | convolution fusion | flops 1074790400 | bytes 12582912 | tf_op jit(solution)/shard_map/hts,the->she/dot_general | solution.py:77
  138.9 2.3 %copy.45 = bf16[1024,512]{1,0:T(8,128)(2,1)} copy(bf16[1024,512]{0,1:T(8,128)(2,1)} %bitcast.68) | data formatting | bytes 2097152
  141.1 2.3 %copy.48 = bf16[1024,512]{1,0:T(8,128)(2,1)} copy(bf16[1024,512]{0,1:T(8,128)(2,1)} %bitcast.65) | data formatting | bytes 2097152
  143.4 2.4 %add_convert_fusion = bf16[4,128,1024]{2,1,0:T(8,128)(2,1)S(1)} fusion(f32[4,128,1024]{2,1,0:T(8,128)} %fusion.38, bf16[1024,4,128]{0,2,1:T(8,128)(2,1)S(1)} %bitcast.60, bf16[4,128,128]{2,1,0:T(8,128)(2,1)S(1)} %collective-permute-done.5, bf16[4,128,128]{2,1,0:T(8,128)(2,1)} %copy-done.2, bf16[4,128,128]{2,1,0:T(8,128)(2,1)} %copy-done.4, ...), kind=kOutput, calls=%fused_computation.7 | convolution fusion | flops 136577024 | bytes 4849749 | tf_op jit(solution)/shard_map/the,hde->thd/dot_general | solution.py:74
  147.2 2.4 %add_convert_fusion.1 = bf16[4,128,1024]{2,1,0:T(8,128)(2,1)S(1)} fusion(f32[4,128,1024]{2,1,0:T(8,128)} %fusion.37, bf16[1024,4,128]{0,2,1:T(8,128)(2,1)S(1)} %bitcast.52, bf16[4,128,128]{2,1,0:T(8,128)(2,1)S(1)} %collective-permute-done, bf16[4,128,128]{2,1,0:T(8,128)(2,1)S(1)} %collective-permute-done.1, bf16[4,128,128]{2,1,0:T(8,128)(2,1)} %copy-done.3, ...), kind=kOutput, calls=%fused_computation.8 | convolution fusion | flops 136577024 | bytes 4849749 | tf_op jit(solution)/shard_map/the,hde->thd/dot_general | solution.py:70
  (60 shorter events, 17.3 us)
Async XLA Ops:
  4.2 5.0 %copy-start.7 = (bf16[1024,512]{1,0:T(8,128)(2,1)S(1)}, bf16[1024,512]{1,0:T(8,128)(2,1)}, u32[]{:S(2)}) copy-start(bf16[1024,512]{1,0:T(8,128)(2,1)} %param.7) | copy-start | bytes 3145732
  4.2 5.5 %copy-start.13 = (f32[4,6]{1,0:T(4,128)S(1)}, f32[4,6]{1,0:T(4,128)}, u32[]{:S(2)}) copy-start(f32[4,6]{1,0:T(4,128)} %param.6) | copy-start | bytes 292
  4.2 54.2 %all-to-all-start = ((bf16[4,1024,512]{2,1,0:T(8,128)(2,1)}), bf16[4,1024,512]{2,1,0:T(8,128)(2,1)}, u32[]{:S(2)}, u32[]{:S(2)}) async-start(bf16[4,1024,512]{2,1,0:T(8,128)(2,1)} %stack.2), calls=%async_computation | async-start | bytes 8388608 | tf_op jit(solution)/shard_map/all_to_all | solution.py:22
  96.4 4.2 %copy-start.12 = (bf16[4,128,128]{2,1,0:T(8,128)(2,1)S(1)}, bf16[4,128,128]{2,1,0:T(8,128)(2,1)}, u32[]{:S(2)}) copy-start(bf16[4,128,128]{2,1,0:T(8,128)(2,1)} %get-tuple-element.23) | copy-start | bytes 393220
  96.4 4.2 %copy-start.11 = (bf16[4,128,128]{2,1,0:T(8,128)(2,1)S(1)}, bf16[4,128,128]{2,1,0:T(8,128)(2,1)}, u32[]{:S(2)}) copy-start(bf16[4,128,128]{2,1,0:T(8,128)(2,1)} %get-tuple-element.21) | copy-start | bytes 393220
  100.7 3.4 %collective-permute-start.5 = (bf16[4,128,128]{2,1,0:T(8,128)(2,1)S(1)}, bf16[4,128,128]{2,1,0:T(8,128)(2,1)S(1)}, u32[]{:S(2)}, u32[]{:S(2)}) collective-permute-start(bf16[4,128,128]{2,1,0:T(8,128)(2,1)S(1)} %copy-done.12), channel_id=1, source_target_pairs={{0,4},{4,0},{8,12},{12,8},{16,20},{20,16},{24,28},{28,24},{32,36},... | collective-permute-start | bytes 393224 | tf_op jit(solution)/shard_map/ppermute | solution.py:11
  100.7 3.4 %copy-start.1 = (f32[4,128,128]{2,1,0:T(8,128)S(1)}, f32[4,128,128]{2,1,0:T(8,128)}, u32[]{:S(2)}) copy-start(f32[4,128,128]{2,1,0:T(8,128)} %get-tuple-element.24) | copy-start | bytes 786436
  100.7 5.1 %copy-start = (f32[4,128,128]{2,1,0:T(8,128)S(1)}, f32[4,128,128]{2,1,0:T(8,128)}, u32[]{:S(2)}) copy-start(f32[4,128,128]{2,1,0:T(8,128)} %get-tuple-element.22) | copy-start | bytes 786436
  100.7 5.1 %collective-permute-start = (bf16[4,128,128]{2,1,0:T(8,128)(2,1)S(1)}, bf16[4,128,128]{2,1,0:T(8,128)(2,1)S(1)}, u32[]{:S(2)}, u32[]{:S(2)}) collective-permute-start(bf16[4,128,128]{2,1,0:T(8,128)(2,1)S(1)} %copy-done.11), channel_id=1, source_target_pairs={{0,4},{4,0},{8,12},{12,8},{16,20},{20,16},{24,28},{28,24},{32,36},... | collective-permute-start | bytes 393224 | tf_op jit(solution)/shard_map/ppermute | solution.py:11
  104.1 30.1 %copy-start.14 = (f32[4]{0:T(128)S(1)}, f32[4]{0:T(128)}, u32[]{:S(2)}) copy-start(f32[4]{0:T(128)} %get-tuple-element.17) | copy-start | bytes 52
  104.2 6.4 %collective-permute-start.6 = (bf16[4,128,128]{2,1,0:T(8,128)(2,1)S(1)}, bf16[4,128,128]{2,1,0:T(8,128)(2,1)S(1)}, u32[]{:S(2)}, u32[]{:S(2)}) collective-permute-start(bf16[4,128,128]{2,1,0:T(8,128)(2,1)S(1)} %fusion.24), channel_id=1, source_target_pairs={{0,8},{4,12},{8,0},{12,4},{16,24},{20,28},{24,16},{28,20},{32,40},... | collective-permute-start | bytes 393224 | tf_op jit(solution)/shard_map/ppermute | solution.py:11
  105.8 8.0 %collective-permute-start.1 = (bf16[4,128,128]{2,1,0:T(8,128)(2,1)S(1)}, bf16[4,128,128]{2,1,0:T(8,128)(2,1)S(1)}, u32[]{:S(2)}, u32[]{:S(2)}) collective-permute-start(bf16[4,128,128]{2,1,0:T(8,128)(2,1)S(1)} %fusion.22), channel_id=1, source_target_pairs={{0,8},{4,12},{8,0},{12,4},{16,24},{20,28},{24,16},{28,20},{32,40},... | collective-permute-start | bytes 393224 | tf_op jit(solution)/shard_map/ppermute | solution.py:11
  110.6 24.2 %copy-start.2 = (bf16[4,128,128]{2,1,0:T(8,128)(2,1)}, bf16[4,128,128]{2,1,0:T(8,128)(2,1)S(1)}, u32[]{:S(2)}) copy-start(bf16[4,128,128]{2,1,0:T(8,128)(2,1)S(1)} %collective-permute-done.6) | copy-start | bytes 393220
  110.7 8.0 %collective-permute-start.7 = (bf16[4,128,128]{2,1,0:T(8,128)(2,1)S(1)}, bf16[4,128,128]{2,1,0:T(8,128)(2,1)S(1)}, u32[]{:S(2)}, u32[]{:S(2)}) collective-permute-start(bf16[4,128,128]{2,1,0:T(8,128)(2,1)S(1)} %fusion.27), channel_id=1, source_target_pairs={{0,16},{4,20},{8,24},{12,28},{16,0},{20,4},{24,8},{28,12},{32,48},... | collective-permute-start | bytes 393224 | tf_op jit(solution)/shard_map/ppermute | solution.py:11
  113.9 6.9 %collective-permute-start.2 = (bf16[4,128,128]{2,1,0:T(8,128)(2,1)S(1)}, bf16[4,128,128]{2,1,0:T(8,128)(2,1)S(1)}, u32[]{:S(2)}, u32[]{:S(2)}) collective-permute-start(bf16[4,128,128]{2,1,0:T(8,128)(2,1)S(1)} %fusion.26), channel_id=1, source_target_pairs={{0,16},{4,20},{8,24},{12,28},{16,0},{20,4},{24,8},{28,12},{32,48},... | collective-permute-start | bytes 393224 | tf_op jit(solution)/shard_map/ppermute | solution.py:11
  118.6 18.6 %copy-start.4 = (bf16[4,128,128]{2,1,0:T(8,128)(2,1)}, bf16[4,128,128]{2,1,0:T(8,128)(2,1)S(1)}, u32[]{:S(2)}) copy-start(bf16[4,128,128]{2,1,0:T(8,128)(2,1)S(1)} %collective-permute-done.7) | copy-start | bytes 393220
  118.7 6.3 %collective-permute-start.8 = (bf16[4,128,128]{2,1,0:T(8,128)(2,1)S(1)}, bf16[4,128,128]{2,1,0:T(8,128)(2,1)S(1)}, u32[]{:S(2)}, u32[]{:S(2)}) collective-permute-start(bf16[4,128,128]{2,1,0:T(8,128)(2,1)S(1)} %fusion.25), channel_id=1, source_target_pairs={{0,32},{4,36},{8,40},{12,44},{16,48},{20,52},{24,56},{28,60},{32,0... | collective-permute-start | bytes 393224 | tf_op jit(solution)/shard_map/ppermute | solution.py:11
  120.8 16.5 %copy-start.3 = (bf16[4,128,128]{2,1,0:T(8,128)(2,1)}, bf16[4,128,128]{2,1,0:T(8,128)(2,1)S(1)}, u32[]{:S(2)}) copy-start(bf16[4,128,128]{2,1,0:T(8,128)(2,1)S(1)} %collective-permute-done.2) | copy-start | bytes 393220
  120.8 8.4 %collective-permute-start.3 = (bf16[4,128,128]{2,1,0:T(8,128)(2,1)S(1)}, bf16[4,128,128]{2,1,0:T(8,128)(2,1)S(1)}, u32[]{:S(2)}, u32[]{:S(2)}) collective-permute-start(bf16[4,128,128]{2,1,0:T(8,128)(2,1)S(1)} %fusion.23), channel_id=1, source_target_pairs={{0,32},{4,36},{8,40},{12,44},{16,48},{20,52},{24,56},{28,60},{32,0... | collective-permute-start | bytes 393224 | tf_op jit(solution)/shard_map/ppermute | solution.py:11
  125.0 12.2 %copy-start.6 = (bf16[4,128,128]{2,1,0:T(8,128)(2,1)}, bf16[4,128,128]{2,1,0:T(8,128)(2,1)S(1)}, u32[]{:S(2)}) copy-start(bf16[4,128,128]{2,1,0:T(8,128)(2,1)S(1)} %collective-permute-done.8) | copy-start | bytes 393220
  125.1 9.1 %collective-permute-start.9 = (bf16[4,128,128]{2,1,0:T(8,128)(2,1)S(1)}, bf16[4,128,128]{2,1,0:T(8,128)(2,1)S(1)}, u32[]{:S(2)}, u32[]{:S(2)}) collective-permute-start(bf16[4,128,128]{2,1,0:T(8,128)(2,1)S(1)} %fusion.21), channel_id=1, source_target_pairs={{0,64},{4,68},{8,72},{12,76},{16,80},{20,84},{24,88},{28,92},{32,9... | collective-permute-start | bytes 393224 | tf_op jit(solution)/shard_map/ppermute | solution.py:11
  129.3 8.0 %copy-start.5 = (bf16[4,128,128]{2,1,0:T(8,128)(2,1)}, bf16[4,128,128]{2,1,0:T(8,128)(2,1)S(1)}, u32[]{:S(2)}) copy-start(bf16[4,128,128]{2,1,0:T(8,128)(2,1)S(1)} %collective-permute-done.3) | copy-start | bytes 393220
  129.4 7.9 %collective-permute-start.4 = (bf16[4,128,128]{2,1,0:T(8,128)(2,1)S(1)}, bf16[4,128,128]{2,1,0:T(8,128)(2,1)S(1)}, u32[]{:S(2)}, u32[]{:S(2)}) collective-permute-start(bf16[4,128,128]{2,1,0:T(8,128)(2,1)S(1)} %fusion.11), channel_id=1, source_target_pairs={{0,64},{4,68},{8,72},{12,76},{16,80},{20,84},{24,88},{28,92},{32,9... | collective-permute-start | bytes 393224 | tf_op jit(solution)/shard_map/ppermute | solution.py:11
  134.2 3.0 %copy-start.10 = (bf16[4,128,128]{2,1,0:T(8,128)(2,1)}, bf16[4,128,128]{2,1,0:T(8,128)(2,1)S(1)}, u32[]{:S(2)}) copy-start(bf16[4,128,128]{2,1,0:T(8,128)(2,1)S(1)} %collective-permute-done.9) | copy-start | bytes 393220
  (2 other events, 4.3 us)
